TPU v7x, 32 devices: a whole 2x2x4 slice. The times are simulated.
32 devices in a mesh: dp: 8 (over y, x, core), tensor: 4 (over z).
Axes of the slice: x: 2, y: 2, z: 4, core: 2. Of those that a mesh axis runs over, the one named last changes fastest.
Arguments:
- tokens: bfloat16 [4096, 3584], P('dp'), may hold values from -6 to 6
- gate_weight: bfloat16 [3584, 10240], P(None, 'tensor'), may hold values from -0.09375 to 0.09375
- up_act: bfloat16 [4096, 10240], P('dp', 'tensor'), may hold values from -6 to 6
- hidden_cot: bfloat16 [4096, 10240], P('dp', 'tensor'), may hold values from -6 to 6
- lag_grads: bfloat16 [8, 3584, 10240], P('dp', None, 'tensor'), may hold values from -8 to 8, as said below
- skip_mask: int32 [8], P('dp'), may hold values 0 or 1
- aggregate: float32 [3584, 10240], P('dp', 'tensor'), may hold values from -3 to 3
Outputs:
- new_aggregate: float32 [3584, 10240], P('dp', 'tensor')
- input_grad: bfloat16 [4096, 3584], P('dp', 'tensor')
- change_rms: float32 [8], P('dp')
Inputs may be any that keep to these rules, and one draw needn't show every extreme that they name: `lag_grads`: real-valued.
All inputs are finite; a program needn't handle non-finite values. No bound on the sum of `skip_mask` on one device may be relied on, other than what follows from the above.
Results may differ from a plain program's by a relative error of at most 0.014.
Values may be sent and summed in bfloat16 or wider, within the bound.
A program may use at most 192 MiB of HBM per device.

v0:
```python
import jax
import jax.numpy as jnp
from jax import lax
from jax.sharding import PartitionSpec as P

D = 3584
FF = 10240
TOK_DEV = 512


clip_level = 0.1


def body(tokens, gate_weight, up_act, hidden_cot, lag_grads, skip_mask, aggregate):
    gate = jnp.dot(tokens, gate_weight, preferred_element_type=jnp.float32)
    sig = jax.nn.sigmoid(gate)
    d_gate = (
        hidden_cot.astype(jnp.float32)
        * up_act.astype(jnp.float32)
        * sig
        * (1.0 + gate * (1.0 - sig))
    ).astype(jnp.bfloat16)
    partial_input = lax.dot_general(
        d_gate, gate_weight, (((1,), (1,)), ((), ())), preferred_element_type=jnp.float32
    )
    input_grad = lax.psum_scatter(
        partial_input.astype(jnp.bfloat16), "tensor", scatter_dimension=1, tiled=True
    )
    inverse = 1.0 / TOK_DEV
    lagged = lag_grads[0]
    grad = (
        lax.dot_general(
            tokens, d_gate, (((0,), (0,)), ((), ())), preferred_element_type=jnp.float32
        )
        * inverse
    )
    change = grad - lagged.astype(jnp.float32)
    total_sq = lax.psum(jnp.sum(change * change), "tensor")
    rms = jnp.sqrt(total_sq / (D * FF) + 1e-06)
    factor = skip_mask[0].astype(jnp.float32) * jnp.minimum(1.0, clip_level / rms)
    sent = (factor * change).astype(jnp.bfloat16)
    summed = lax.psum_scatter(sent, "dp", scatter_dimension=0, tiled=True).astype(jnp.float32)
    return (aggregate + summed, input_grad, rms.reshape(1))


def solution(mesh):
    return jax.shard_map(
        body,
        mesh=mesh,
        in_specs=(
            P("dp", None),
            P(None, "tensor"),
            P("dp", "tensor"),
            P("dp", "tensor"),
            P("dp", None, "tensor"),
            P("dp"),
            P("dp", "tensor"),
        ),
        out_specs=(P("dp", "tensor"), P("dp", "tensor"), P("dp")),
        check_vma=False,
    )
```

profile of v0, /device:TPU:0, one launch (start us, length us, event | category | flops | bytes accessed | tf_op | source)
XLA Modules:
  0.0 307.0 jit_solution(989033938793674842)
XLA Ops:
  7.2 0.0 copy-start
  7.2 0.0 reduce-scatter.9.cloned.1.call-start
  7.2 16.2 %fusion.4 = f32[512,2560]{1,0:T(8,128)} fusion(bf16[512,3584]{1,0:T(8,128)(2,1)} %param.7, bf16[3584,2560]{1,0:T(8,128)(2,1)} %param.8), kind=kOutput, calls=%fused_computation.10 | convolution fusion | flops 9395240960 | bytes 27262976 | tf_op jit(solution)/shard_map/dot_general | solution.py:15
  23.4 0.0 copy-done
  23.4 19.8 %convolution_convert_fusion = bf16[512,3584]{1,0:T(8,128)(2,1)} fusion(bf16[3584,2560]{1,0:T(8,128)(2,1)} %param.8, f32[512,2560]{1,0:T(8,128)} %fusion.4, bf16[512,2560]{1,0:T(8,128)(2,1)S(1)} %copy-done, bf16[512,2560]{1,0:T(8,128)(2,1)} %param.10), kind=kOutput, calls=%fused_computation.3 | convolution fusion | flops 9412804608 | bytes 32505856 | tf_op jit(solution)/shard_map/dot_general | solution.py:23
  43.2 5.9 %copy.18 = bf16[512,3584]{0,1:T(8,128)(2,1)} copy(bf16[512,3584]{1,0:T(8,128)(2,1)} %convolution_convert_fusion) | data formatting | bytes 7340032
  49.1 0.0 reduce-scatter.9.cloned.1.call-update
  49.1 0.2 reduce-scatter.7.cloned.1.call-start
  49.4 23.2 %copy.13 = bf16[1,3584,2560]{1,2,0:T(8,128)(2,1)} copy(bf16[1,3584,2560]{2,1,0:T(8,128)(2,1)} %param.11) | data formatting | bytes 36700160 | tf_op args[4]
  72.6 30.3 %multiply_reduce_fusion = (f32[]{:T(128)}, f32[3584,2560]{0,1:T(8,128)}) fusion(bf16[1,3584,2560]{1,2,0:T(8,128)(2,1)} %copy.13, bf16[512,3584]{1,0:T(8,128)(2,1)} %param.7, f32[512,2560]{1,0:T(8,128)} %fusion.4, bf16[512,2560]{1,0:T(8,128)(2,1)S(1)} %copy-done, bf16[512,2560]{1,0:T(8,128)(2,1)} %param.10), kind=kOutput, calls=%fused_computation.2 | convolution fusion | flops 9456844800 | bytes 69206016 | tf_op jit(solution)/shard_map/dot_general | solution.py:32
  103.0 14.8 %psum.7 = f32[]{:T(128)} all-reduce(f32[]{:T(128)} %get-tuple-element.9), channel_id=1, replica_groups=mesh['dp'=8,'tensor'=4] {'tensor'}, use_global_device_ids=true, to_apply=%region_1.0 | all-reduce | flops 1 | bytes 8 | tf_op jit(solution)/shard_map/psum | solution.py:38
  119.2 20.2 %multiply_convert_fusion = bf16[3584,2560]{0,1:T(8,128)(2,1)} fusion(f32[3584,2560]{0,1:T(8,128)} %get-tuple-element.10, f32[]{:T(128)S(6)} %mul.41), kind=kLoop, calls=%fused_computation.1 | loop fusion | flops 18350080 | bytes 55050244 | tf_op jit(solution)/shard_map/convert_element_type | solution.py:41
  139.3 23.4 %copy.16 = bf16[3584,2560]{1,0:T(8,128)(2,1)} copy(bf16[3584,2560]{0,1:T(8,128)(2,1)} %multiply_convert_fusion) | data formatting | bytes 36700160
  162.8 0.0 reduce-scatter.7.cloned.1.call-update
  162.8 6.1 %copy.14 = f32[448,2560]{0,1:T(8,128)} copy(f32[448,2560]{1,0:T(8,128)} %param.13) | data formatting | bytes 9175040 | tf_op args[6]
  168.9 0.0 reduce-scatter.9.cloned.1.call-done
  168.9 2.4 copy.19
  171.3 113.5 %reduce-scatter.7.cloned.1.call-done = bf16[448,2560]{1,0:T(8,128)(2,1)} async-done(((bf16[3584,2560]{1,0:T(8,128)(2,1)}), bf16[448,2560]{1,0:T(8,128)(2,1)}) %reduce-scatter.7.cloned.1.call-update) | async-done | bytes 2293776
  284.8 2.9 copy.17
  287.7 5.6 %convert_add_fusion = f32[448,2560]{0,1:T(8,128)} fusion(f32[448,2560]{0,1:T(8,128)} %copy.14, bf16[448,2560]{0,1:T(8,128)(2,1)S(1)} %copy.17), kind=kLoop, calls=%fused_computation.4 | loop fusion | flops 2293760 | bytes 11468800 | tf_op jit(solution)/shard_map/add | solution.py:43
  293.3 5.7 %copy.15 = f32[448,2560]{1,0:T(8,128)} copy(f32[448,2560]{0,1:T(8,128)} %convert_add_fusion) | data formatting | bytes 9175040
Async XLA Ops:
  7.2 16.2 %copy-start = (bf16[512,2560]{1,0:T(8,128)(2,1)S(1)}, bf16[512,2560]{1,0:T(8,128)(2,1)}, u32[]{:S(2)}) copy-start(bf16[512,2560]{1,0:T(8,128)(2,1)} %param.9) | copy-start | bytes 7864324
  7.2 161.7 %reduce-scatter.9.cloned.1.call-start = ((), (), s32[]{:S(2)}) async-start(), calls=%async_computation.3 | async-start | bytes 4587520
  49.1 235.6 %reduce-scatter.7.cloned.1.call-start = ((), (), s32[]{:S(2)}) async-start(), calls=%async_computation.2 | async-start | bytes 20643840
Sparse Core Ops, SparseCore 0:
  49.3 71.4 reduce-scatter.8
  162.9 121.8 reduce-scatter.6
where the time goes:
time: 309 us; the launch traced here: 307 us
  waiting for transfers between devices  114 us (37%)
  local copies, waits for them, and re-layouts  69.7 us (23%)
  matrix products  66.3 us (21%)
  other arithmetic  25.8 us (8%)
  between operations  16.6 us (5%)
  blocking collectives  14.8 us (5%)
    unnamed x4, waiting for transfers between devices  114 us
    unnamed x9, local copies, waits for them, and re-layouts  69.7 us
    dot_general x1, matrix products, body(): lax.dot_general(tokens, d_gate, (((0,), (0,)), ((), ())), preferred_eleme...  30.3 us
    convert_element_type x1, other arithmetic, body(): sent = (factor * change).astype(jnp.bfloat16)  20.2 us
    dot_general x1, matrix products, body(): lax.dot_general(d_gate, gate_weight, (((1,), (1,)), ((), ())), preferred_...  19.8 us
    dot_general x1, matrix products, body(): gate = jnp.dot(tokens, gate_weight, preferred_element_type=jnp.float32)  16.2 us
    psum x1, blocking collectives, body(): total_sq = lax.psum(jnp.sum(change * change), 'tensor')  14.8 us
  transfers between devices with their start and end apart: 2, of which 1 were waited for; matrix products, arithmetic and copies ran while one was open for 34% of the time, Pallas kernels for 0%

commit v1 on v0

v1 whole, which is shorter than its diff:
```python
import functools

import jax
import jax.numpy as jnp
from jax import lax
from jax.experimental import pallas as pl
from jax.experimental.pallas import tpu as pltpu
from jax.sharding import PartitionSpec as P

MESH = pl.DeviceIdType.MESH
clip_level = 0.1
F32 = jnp.float32
BF16 = jnp.bfloat16


def pick(size, options):
    for option in options:
        if size % option == 0:
            return option
    return size


def kernel(cfg, x_ref, g_ref, mask_ref, lag_ref, w_ref, out_ref, ig_ref, rms_ref,
           xt, chg, r1, a1, a2, b1, b2, stream, pi, pir, acc, stat, statr,
           lsem, r1s, r1r, a1s, a1r, a2s, a2r, b1s, b1r, b2s, b2r, pis, pir_s, sts, strr):
    NX, NY, T, D, FF = cfg
    NC = NX * NY
    tok, F = g_ref.shape
    R = chg.shape[2]
    FH = F // 2
    CH = pi.shape[2]
    inverse = 1.0 / tok
    dp = lax.axis_index("dp")
    t = lax.axis_index("tensor")
    core = lax.rem(dp, 2)
    chip = dp // 2
    x = lax.rem(chip, NX)
    y = chip // NX

    def chip_at(xx, yy):
        return lax.rem(xx, NX) + NX * lax.rem(yy, NY)

    def peer(cc):
        return (2 * cc + core, t)

    partner = (2 * chip + 1 - core, t)

    barrier = pltpu.get_barrier_semaphore()
    peers = []
    for m in range(T):
        for c in range(2):
            if m or c:
                peers.append((2 * chip + (core if c == 0 else 1 - core), lax.rem(t + m, T)))
    for k in range(1, NX):
        peers.append(peer(chip_at(x + k, y)))
    for k in range(1, NY):
        peers.append(peer(chip_at(x, y + k)))
    for p in peers:
        pl.semaphore_signal(barrier, inc=1, device_id=p, device_id_type=MESH)

    def remote(src, dst, ss, rs, dev):
        return pltpu.make_async_remote_copy(
            src_ref=src, dst_ref=dst, send_sem=ss, recv_sem=rs, device_id=dev, device_id_type=MESH
        )

    def dest(i):
        own = i // NC
        cc = lax.rem(chip + 1 + lax.rem(i, NC), NC)
        par = own * core + (1 - own) * (1 - core)
        return cc, par

    def lag_copy(i):
        cc, par = dest(i)
        row = pl.multiple_of((2 * cc + par) * R, 8)
        slot = lax.rem(i, 2)
        return pltpu.make_async_copy(
            lag_ref.at[0, pl.ds(row, R), :], stream.at[slot, pl.ds(0, R), :], lsem.at[slot]
        )

    lag_copy(jnp.int32(0)).start()
    acc[...] = jnp.zeros_like(acc)
    XB = pick(D, (512, 256, 128))

    def transpose(k, _):
        o = pl.multiple_of(k * XB, XB)
        xt[pl.ds(o, XB), :] = x_ref[:, pl.ds(o, XB)].T
        return 0

    lax.fori_loop(0, D // XB, transpose, 0)
    pl.semaphore_wait(barrier, len(peers))

    NB = pick(F, (512, 256, 128))

    def r1_copy(cc):
        return remote(chg.at[cc, 1 - core], r1.at[cc], r1s.at[cc], r1r.at[cc], partner)

    def change_step(i, send, last):
        cc, par = dest(i)
        row = pl.multiple_of((2 * cc + par) * R, 8)
        slot = lax.rem(i, 2)
        if not last:
            lag_copy(i + 1).start()
        lag_copy(i).wait()
        left = xt[pl.ds(row, R), :]

        def tile(n, _):
            o = pl.multiple_of(n * NB, NB)
            g = jnp.dot(left, g_ref[:, pl.ds(o, NB)], preferred_element_type=F32) * inverse
            ch = g - stream[slot, pl.ds(0, R), pl.ds(o, NB)].astype(F32)
            acc[...] += (ch * ch).reshape(R // 8, 8, NB).sum(0)
            chg[cc, par, :, pl.ds(o, NB)] = ch.astype(BF16)
            return 0

        lax.fori_loop(0, F // NB, tile, 0)
        if send:
            r1_copy(cc).start()

    def send_step(i, _):
        change_step(i, True, False)
        return 0

    def own_step(i, _):
        change_step(i, False, False)
        return 0

    lax.fori_loop(0, NC, send_step, 0)
    lax.fori_loop(NC, 2 * NC - 1, own_step, 0)
    change_step(jnp.int32(2 * NC - 1), False, True)

    def w_copy(i):
        m, h = i // 2, lax.rem(i, 2)
        owner = lax.rem(t + 1 + m, T)
        row = pl.multiple_of(owner * (2 * CH) + h * CH, 8)
        return pltpu.make_async_copy(
            w_ref.at[pl.ds(row, CH), :], stream.at[h, pl.ds(0, CH), :], lsem.at[h]
        )

    w_copy(jnp.int32(0)).start()
    w_copy(jnp.int32(1)).start()

    total = jnp.sum(jnp.sum(acc[...], axis=1, keepdims=True), axis=0, keepdims=True)
    stat[0] = jnp.broadcast_to(total, (8, 128))
    stat[1] = jnp.full((8, 128), mask_ref[0].astype(F32), F32)
    stat_copies = []
    for m in range(T):
        for c in range(2):
            if m or c:
                n = 2 * m + c - 1
                stat_copies.append(remote(
                    stat, statr.at[n], sts.at[n], strr.at[n],
                    (2 * chip + (core if c == 0 else 1 - core), lax.rem(t + m, T))))
    for copy in stat_copies:
        copy.start()
    for copy in stat_copies:
        copy.wait()
    own_sq = stat[0]
    for m in range(1, T):
        own_sq = own_sq + statr[2 * m - 1, 0]
    par_sq = statr[0, 0]
    for m in range(1, T):
        par_sq = par_sq + statr[2 * m, 0]

    def rms_of(sq):
        return jnp.sqrt(sq / (D * FF) + 1e-06)

    rms_own = rms_of(own_sq)
    rms_ref[...] = rms_own
    f_own = (stat[1] * jnp.minimum(1.0, clip_level / rms_own))[0:1, 0:1]
    f_par = (statr[0, 1] * jnp.minimum(1.0, clip_level / rms_of(par_sq)))[0:1, 0:1]

    def r1_wait(cc, _):
        r1_copy(cc).wait()
        return 0

    lax.fori_loop(0, NC, r1_wait, 0)

    RB = pick(R, (64, 32, 16))

    def combine(cc, half, arrived, final):
        cols = pl.ds(half * FH, FH)

        def rows(i, _):
            rr = pl.ds(pl.multiple_of(i * RB, RB), RB)
            v = chg[cc, core, rr, cols].astype(F32) * f_own + r1[cc, rr, cols].astype(F32) * f_par
            for ref in arrived:
                v = v + ref[rr, :].astype(F32)
            if final:
                out_ref[rr, cols] = v.astype(BF16)
            else:
                chg[cc, core, rr, cols] = v.astype(BF16)
            return 0

        lax.fori_loop(0, R // RB, rows, 0)

    def half_of(cc, half):
        return chg.at[cc, core, :, pl.ds(half * FH, FH)]

    a1c, b1c, a2c, b2c = {}, {}, {}, {}

    def send_a1(k, j):
        cc = chip_at(x + k, y + j)
        combine(cc, 0, (), False)
        n = (k - 1) * NY + j
        a1c[k, j] = remote(half_of(cc, 0), a1.at[n], a1s.at[n], a1r.at[n], peer(chip_at(x + k, y)))
        a1c[k, j].start()

    def send_b1(k, j):
        cc = chip_at(x + j, y + k)
        combine(cc, 1, (), False)
        n = (k - 1) * NX + j
        b1c[k, j] = remote(half_of(cc, 1), b1.at[n], b1s.at[n], b1r.at[n], peer(chip_at(x, y + k)))
        b1c[k, j].start()

    order_a = [(k, j) for j in list(range(1, NY)) + [0] for k in range(1, NX)]
    order_b = [(k, j) for j in list(range(1, NX)) + [0] for k in range(1, NY)]
    for n in range(max(len(order_a), len(order_b))):
        if n < len(order_a):
            send_a1(*order_a[n])
        if n < len(order_b):
            send_b1(*order_b[n])

    def pi_copy(m, h):
        n = 2 * m + h
        return remote(pi.at[n], pir.at[n], pis.at[n], pir_s.at[n], (dp, lax.rem(t + 1 + m, T)))

    def pi_step(i, send, more):
        m, h = i // 2, lax.rem(i, 2)
        w_copy(i).wait()
        pi[i] = lax.dot_general(
            g_ref[...], stream[h, pl.ds(0, CH), :], (((1,), (1,)), ((), ())), preferred_element_type=F32
        ).astype(BF16)
        if more:
            w_copy(i + 2).start()
        if send:
            pi_copy(m, h).start()

    def pi_send(i, _):
        pi_step(i, True, True)
        return 0

    lax.fori_loop(0, 2 * (T - 1), pi_send, 0)

    def pi_own(i, _):
        pi_step(i, False, False)
        return 0

    lax.fori_loop(2 * (T - 1), 2 * T, pi_own, 0)

    for j in range(1, NY):
        for k in range(1, NX):
            a1c[k, j].wait()
        cc = chip_at(x, y + j)
        combine(cc, 0, [a1.at[(k - 1) * NY + j] for k in range(1, NX)], False)
        a2c[j] = remote(half_of(cc, 0), a2.at[j - 1], a2s.at[j - 1], a2r.at[j - 1], peer(cc))
        a2c[j].start()
    for j in range(1, NX):
        for k in range(1, NY):
            b1c[k, j].wait()
        cc = chip_at(x + j, y)
        combine(cc, 1, [b1.at[(k - 1) * NX + j] for k in range(1, NY)], False)
        b2c[j] = remote(half_of(cc, 1), b2.at[j - 1], b2s.at[j - 1], b2r.at[j - 1], peer(cc))
        b2c[j].start()

    for m in range(T - 1):
        for h in range(2):
            pi_copy(m, h).wait()
    TB = pick(tok, (64, 32, 16))
    for h in range(2):
        def ig_rows(i, _):
            rr = pl.ds(pl.multiple_of(i * TB, TB), TB)
            v = pi[2 * (T - 1) + h, rr, :].astype(F32)
            for m in range(T - 1):
                v = v + pir[2 * m + h, rr, :].astype(F32)
            ig_ref[rr, pl.ds(h * CH, CH)] = v.astype(BF16)
            return 0

        lax.fori_loop(0, tok // TB, ig_rows, 0)

    for k in range(1, NX):
        a1c[k, 0].wait()
    for j in range(1, NY):
        a2c[j].wait()
    combine(chip, 0, [a1.at[(k - 1) * NY] for k in range(1, NX)] + [a2.at[j - 1] for j in range(1, NY)], True)
    for k in range(1, NY):
        b1c[k, 0].wait()
    for j in range(1, NX):
        b2c[j].wait()
    combine(chip, 1, [b1.at[(k - 1) * NX] for k in range(1, NY)] + [b2.at[j - 1] for j in range(1, NX)], True)


def body(cfg, tokens, gate_weight, up_act, hidden_cot, lag_grads, skip_mask, aggregate):
    NX, NY, T, D, FF = cfg
    NC = NX * NY
    gate = jnp.dot(tokens, gate_weight, preferred_element_type=F32)
    sig = jax.nn.sigmoid(gate)
    d_gate = (
        hidden_cot.astype(F32) * up_act.astype(F32) * sig * (1.0 + gate * (1.0 - sig))
    ).astype(BF16)
    tok, F = d_gate.shape
    R = D // (2 * NC)
    CH = D // T // 2
    FH = F // 2
    NB = pick(F, (512, 256, 128))
    nA, nB = (NX - 1) * NY, (NY - 1) * NX
    vmem = pl.BlockSpec(memory_space=pltpu.VMEM)
    hbm = pl.BlockSpec(memory_space=pl.ANY)
    dma = pltpu.SemaphoreType.DMA
    summed, input_grad, rms = pl.pallas_call(
        functools.partial(kernel, cfg),
        out_shape=(
            jax.ShapeDtypeStruct((R, F), BF16),
            jax.ShapeDtypeStruct((tok, 2 * CH), BF16),
            jax.ShapeDtypeStruct((8, 128), F32),
        ),
        in_specs=[vmem, vmem, pl.BlockSpec(memory_space=pltpu.SMEM), hbm, hbm],
        out_specs=(vmem, vmem, vmem),
        scratch_shapes=[
            pltpu.VMEM((D, tok), BF16),
            pltpu.VMEM((NC, 2, R, F), BF16),
            pltpu.VMEM((NC, R, F), BF16),
            pltpu.VMEM((nA, R, FH), BF16),
            pltpu.VMEM((NY - 1, R, FH), BF16),
            pltpu.VMEM((nB, R, FH), BF16),
            pltpu.VMEM((NX - 1, R, FH), BF16),
            pltpu.VMEM((2, max(R, CH), F), BF16),
            pltpu.VMEM((2 * T, tok, CH), BF16),
            pltpu.VMEM((2 * (T - 1), tok, CH), BF16),
            pltpu.VMEM((8, NB), F32),
            pltpu.VMEM((2, 8, 128), F32),
            pltpu.VMEM((2 * T - 1, 2, 8, 128), F32),
            dma((2,)),
            dma((NC,)), dma((NC,)),
            dma((nA,)), dma((nA,)),
            dma((NY - 1,)), dma((NY - 1,)),
            dma((nB,)), dma((nB,)),
            dma((NX - 1,)), dma((NX - 1,)),
            dma((2 * (T - 1),)), dma((2 * (T - 1),)),
            dma((2 * T - 1,)), dma((2 * T - 1,)),
        ],
        compiler_params=pltpu.CompilerParams(
            collective_id=0, has_side_effects=True, vmem_limit_bytes=67043328
        ),
    )(tokens, d_gate, skip_mask, lag_grads, gate_weight)
    return (aggregate + summed.astype(F32), input_grad, rms[0, 0:1])


def solution(mesh):
    dp, tensor = mesh.shape["dp"], mesh.shape["tensor"]

    def whole(tokens, gate_weight, *rest):
        D, FF = gate_weight.shape
        cfg = (2, dp // 4, tensor, D, FF)
        return jax.shard_map(
            functools.partial(body, cfg),
            mesh=mesh,
            in_specs=(
                P("dp", None),
                P(None, "tensor"),
                P("dp", "tensor"),
                P("dp", "tensor"),
                P("dp", None, "tensor"),
                P("dp"),
                P("dp", "tensor"),
            ),
            out_specs=(P("dp", "tensor"), P("dp", "tensor"), P("dp")),
            check_vma=False,
        )(tokens, gate_weight, *rest)

    return whole
```

time: 309 us -> 156 us (0.50)
  the two profiles are of different devices: /device:TPU:0 before, /device:TPU:11 now
where the time goes in v1:
time: 156 us
  Pallas kernels  129 us (83%)
  matrix products  17.8 us (11%)
  other arithmetic  5.88 us (4%)
  local copies, waits for them, and re-layouts  2.12 us (1%)
    pallas_call x1, Pallas kernels, body(): pl.pallas_call(functools.partial(kernel, cfg), out_shape=(jax.ShapeDtypeS...  129 us
    dot_general x1, matrix products, body(): gate = jnp.dot(tokens, gate_weight, preferred_element_type=F32)  17.8 us
    add x1, other arithmetic, body(): return (aggregate + summed.astype(F32), input_grad, rms[0, 0:1])  5.88 us

profile of v1, /device:TPU:11, one launch (start us, length us, event | category | flops | bytes accessed | tf_op | source)
XLA Modules:
  0.0 155.7 jit_solution(4677950994906389513)
XLA Ops:
  1.3 17.8 %multiply_convert_fusion.g_ref = bf16[512,2560]{1,0:T(8,128)(2,1)} fusion(bf16[512,2560]{1,0:T(8,128)(2,1)} %param.9, bf16[512,2560]{1,0:T(8,128)(2,1)} %param.10, bf16[512,3584]{1,0:T(8,128)(2,1)} %x_ref.1, bf16[3584,2560]{1,0:T(8,128)(2,1)} %w_ref.1), kind=kOutput, calls=%fused_computation | convolution fusion | flops 9410969600 | bytes 29884416 | tf_op jit(solution)/shard_map/dot_general | solution.py:294
  19.1 128.6 %shard_map.94 = (bf16[448,2560]{1,0:T(8,128)(2,1)}, bf16[512,896]{1,0:T(8,128)(2,1)}, f32[8,128]{1,0:T(8,128)}) custom-call(bf16[512,3584]{1,0:T(8,128)(2,1)} %x_ref.1, bf16[512,2560]{1,0:T(8,128)(2,1)} %multiply_convert_fusion.g_ref, s32[1]{0:T(128)S(6)} %copy.11.mask_ref, bf16[1,3584,2560]{2,1,0:T(8,128)(2,1)} %lag_ref.1, bf16[3584,2560]{1,0:T(8,128)(2,1)} %w_ref.1), custom_call_target="tpu_custom_call" | custom-call | tf_op jit(solution)/shard_map/pallas_call | solution.py:308
  147.7 1.2 slice.3
  148.9 0.0 copy-start
  148.9 5.9 %convert_add_fusion = f32[448,2560]{1,0:T(8,128)} fusion(f32[448,2560]{1,0:T(8,128)} %param.13, bf16[448,2560]{1,0:T(8,128)(2,1)} %get-tuple-element.6), kind=kLoop, calls=%fused_computation.1 | loop fusion | flops 2293760 | bytes 11468800 | tf_op jit(solution)/shard_map/add | solution.py:344
  154.8 0.0 copy-done
  154.8 0.9 copy.12
Async XLA Ops:
  148.9 5.9 %copy-start = (bf16[512,896]{1,0:T(8,128)(2,1)S(1)}, bf16[512,896]{1,0:T(8,128)(2,1)}, u32[]{:S(2)}) copy-start(bf16[512,896]{1,0:T(8,128)(2,1)} %get-tuple-element.13) | copy-start | bytes 2752516

commit v2 on v1

--- a/solution.py
+++ b/solution.py
@@ -21,8 +21,8 @@
 
 
 def kernel(cfg, x_ref, g_ref, mask_ref, lag_ref, w_ref, out_ref, ig_ref, rms_ref,
-           xt, chg, r1, a1, a2, b1, b2, stream, pi, pir, acc, stat, statr,
-           lsem, r1s, r1r, a1s, a1r, a2s, a2r, b1s, b1r, b2s, b2r, pis, pir_s, sts, strr):
+           xt, chg, r1, a1, a2, b1, b2, stream, pi, zr, acc, stat, statr,
+           lsem, r1s, r1r, a1s, a1r, a2s, a2r, b1s, b1r, b2s, b2r, zs, zrs, sts, strr):
     NX, NY, T, D, FF = cfg
     NC = NX * NY
     tok, F = g_ref.shape
@@ -127,10 +127,12 @@
     lax.fori_loop(NC, 2 * NC - 1, own_step, 0)
     change_step(jnp.int32(2 * NC - 1), False, True)
 
+    def owner_at(i):
+        return jnp.where(2 * t < T, T - 1 - i // 2, i // 2)
+
     def w_copy(i):
-        m, h = i // 2, lax.rem(i, 2)
-        owner = lax.rem(t + 1 + m, T)
-        row = pl.multiple_of(owner * (2 * CH) + h * CH, 8)
+        h = lax.rem(i, 2)
+        row = pl.multiple_of(owner_at(i) * (2 * CH) + h * CH, 8)
         return pltpu.make_async_copy(
             w_ref.at[pl.ds(row, CH), :], stream.at[h, pl.ds(0, CH), :], lsem.at[h]
         )
@@ -219,32 +221,75 @@
         if n < len(order_b):
             send_b1(*order_b[n])
 
-    def pi_copy(m, h):
-        n = 2 * m + h
-        return remote(pi.at[n], pir.at[n], pis.at[n], pir_s.at[n], (dp, lax.rem(t + 1 + m, T)))
-
-    def pi_step(i, send, more):
-        m, h = i // 2, lax.rem(i, 2)
+    def z_copy(owner, h):
+        nxt = jnp.where(owner > t, t + 1, t - 1)
+        slot = jnp.where((owner < t) & (owner == nxt), T, owner)
+        return remote(
+            pi.at[2 * owner + h], zr.at[2 * slot + h], zs.at[2 * owner + h], zrs.at[2 * slot + h], (dp, nxt)
+        )
+
+    def z_arrived(slot, h):
+        remote(
+            pi.at[h], zr.at[2 * slot + h], zs.at[h], zrs.at[2 * slot + h], (dp, lax.rem(t + 1, T))
+        ).wait_recv()
+
+    TB = pick(tok, (64, 32, 16))
+
+    def z_add(owner, slot, h):
+        z_arrived(slot, h)
+
+        def rows(i, _):
+            rr = pl.ds(pl.multiple_of(i * TB, TB), TB)
+            v = pi[2 * owner + h, rr, :].astype(F32) + zr[2 * slot + h, rr, :].astype(F32)
+            pi[2 * owner + h, rr, :] = v.astype(BF16)
+            return 0
+
+        lax.fori_loop(0, tok // TB, rows, 0)
+
+    def z_relay(owner):
+        for h in range(2):
+            z_add(owner, owner, h)
+            z_copy(owner, h).start()
+
+    at_end = (t == 0) | (t == T - 1)
+
+    def pi_step(i, more):
+        h = lax.rem(i, 2)
+        owner = owner_at(i)
         w_copy(i).wait()
-        pi[i] = lax.dot_general(
+        pi[2 * owner + h] = lax.dot_general(
             g_ref[...], stream[h, pl.ds(0, CH), :], (((1,), (1,)), ((), ())), preferred_element_type=F32
         ).astype(BF16)
         if more:
             w_copy(i + 2).start()
-        if send:
-            pi_copy(m, h).start()
-
-    def pi_send(i, _):
-        pi_step(i, True, True)
-        return 0
-
-    lax.fori_loop(0, 2 * (T - 1), pi_send, 0)
-
-    def pi_own(i, _):
-        pi_step(i, False, False)
-        return 0
-
-    lax.fori_loop(2 * (T - 1), 2 * T, pi_own, 0)
+
+        @pl.when(at_end & (owner != t))
+        def _():
+            z_copy(owner, h).start()
+
+    def pi_more(i, _):
+        pi_step(i, True)
+        return 0
+
+    lax.fori_loop(0, 2 * (T - 1), pi_more, 0)
+
+    def pi_last(i, _):
+        pi_step(i, False)
+        return 0
+
+    lax.fori_loop(2 * (T - 1), 2 * T, pi_last, 0)
+
+    for u in range(1, T - 1):
+        right = T - 1 - (u - t)
+        left = u - (T - 1 - t)
+
+        @pl.when((t > 0) & (u >= t) & (right > t))
+        def _():
+            z_relay(right)
+
+        @pl.when((t < T - 1) & (left >= 0) & (left < t))
+        def _():
+            z_relay(left)
 
     for j in range(1, NY):
         for k in range(1, NX):
@@ -261,20 +306,23 @@
         b2c[j] = remote(half_of(cc, 1), b2.at[j - 1], b2s.at[j - 1], b2r.at[j - 1], peer(cc))
         b2c[j].start()
 
-    for m in range(T - 1):
+    @pl.when(t > 0)
+    def _():
         for h in range(2):
-            pi_copy(m, h).wait()
-    TB = pick(tok, (64, 32, 16))
+            z_add(t, t, h)
+
+    @pl.when(t < T - 1)
+    def _():
+        for h in range(2):
+            z_add(t, T, h)
+
     for h in range(2):
-        def ig_rows(i, _):
-            rr = pl.ds(pl.multiple_of(i * TB, TB), TB)
-            v = pi[2 * (T - 1) + h, rr, :].astype(F32)
-            for m in range(T - 1):
-                v = v + pir[2 * m + h, rr, :].astype(F32)
-            ig_ref[rr, pl.ds(h * CH, CH)] = v.astype(BF16)
-            return 0
-
-        lax.fori_loop(0, tok // TB, ig_rows, 0)
+        ig_ref[:, pl.ds(h * CH, CH)] = pi[2 * t + h]
+    for owner in range(T):
+        @pl.when(owner != t)
+        def _():
+            for h in range(2):
+                z_copy(owner, h).wait_send()
 
     for k in range(1, NX):
         a1c[k, 0].wait()
@@ -324,7 +372,7 @@
             pltpu.VMEM((NX - 1, R, FH), BF16),
             pltpu.VMEM((2, max(R, CH), F), BF16),
             pltpu.VMEM((2 * T, tok, CH), BF16),
-            pltpu.VMEM((2 * (T - 1), tok, CH), BF16),
+            pltpu.VMEM((2 * (T + 1), tok, CH), BF16),
             pltpu.VMEM((8, NB), F32),
             pltpu.VMEM((2, 8, 128), F32),
             pltpu.VMEM((2 * T - 1, 2, 8, 128), F32),
@@ -334,7 +382,7 @@
             dma((NY - 1,)), dma((NY - 1,)),
             dma((nB,)), dma((nB,)),
             dma((NX - 1,)), dma((NX - 1,)),
-            dma((2 * (T - 1),)), dma((2 * (T - 1),)),
+            dma((2 * T,)), dma((2 * (T + 1),)),
             dma((2 * T - 1,)), dma((2 * T - 1,)),
         ],
         compiler_params=pltpu.CompilerParams(

time: 156 us -> 137 us (0.88)
  the two profiles are of different devices: /device:TPU:11 before, /device:TPU:0 now
where the time goes in v2:
time: 137 us
  Pallas kernels  110 us (80%)
  matrix products  17.8 us (13%)
  other arithmetic  5.88 us (4%)
  local copies, waits for them, and re-layouts  2.12 us (2%)
    pallas_call x1, Pallas kernels, body(): pl.pallas_call(functools.partial(kernel, cfg), out_shape=(jax.ShapeDtypeS...  110 us
    dot_general x1, matrix products, body(): gate = jnp.dot(tokens, gate_weight, preferred_element_type=F32)  17.8 us
    add x1, other arithmetic, body(): return (aggregate + summed.astype(F32), input_grad, rms[0, 0:1])  5.88 us

profile of v2, /device:TPU:0, one launch (start us, length us, event | category | flops | bytes accessed | tf_op | source)
XLA Modules:
  0.0 137.2 jit_solution(12923685500458377440)
XLA Ops:
  1.3 17.8 %multiply_convert_fusion.g_ref = bf16[512,2560]{1,0:T(8,128)(2,1)} fusion(bf16[512,2560]{1,0:T(8,128)(2,1)} %param.9, bf16[512,2560]{1,0:T(8,128)(2,1)} %param.10, bf16[512,3584]{1,0:T(8,128)(2,1)} %x_ref.1, bf16[3584,2560]{1,0:T(8,128)(2,1)} %w_ref.1), kind=kOutput, calls=%fused_computation | convolution fusion | flops 9410969600 | bytes 29884416 | tf_op jit(solution)/shard_map/dot_general | solution.py:342
  19.1 110.1 %shard_map.94 = (bf16[448,2560]{1,0:T(8,128)(2,1)}, bf16[512,896]{1,0:T(8,128)(2,1)}, f32[8,128]{1,0:T(8,128)}) custom-call(bf16[512,3584]{1,0:T(8,128)(2,1)} %x_ref.1, bf16[512,2560]{1,0:T(8,128)(2,1)} %multiply_convert_fusion.g_ref, s32[1]{0:T(128)S(6)} %copy.11.mask_ref, bf16[1,3584,2560]{2,1,0:T(8,128)(2,1)} %lag_ref.1, bf16[3584,2560]{1,0:T(8,128)(2,1)} %w_ref.1), custom_call_target="tpu_custom_call" | custom-call | tf_op jit(solution)/shard_map/pallas_call | solution.py:356
  129.2 1.2 slice.3
  130.4 0.0 copy-start
  130.4 5.9 %convert_add_fusion = f32[448,2560]{1,0:T(8,128)} fusion(f32[448,2560]{1,0:T(8,128)} %param.13, bf16[448,2560]{1,0:T(8,128)(2,1)} %get-tuple-element.6), kind=kLoop, calls=%fused_computation.1 | loop fusion | flops 2293760 | bytes 11468800 | tf_op jit(solution)/shard_map/add | solution.py:392
  136.3 0.0 copy-done
  136.3 0.9 copy.12
Async XLA Ops:
  130.4 5.9 %copy-start = (bf16[512,896]{1,0:T(8,128)(2,1)S(1)}, bf16[512,896]{1,0:T(8,128)(2,1)}, u32[]{:S(2)}) copy-start(bf16[512,896]{1,0:T(8,128)(2,1)} %get-tuple-element.13) | copy-start | bytes 2752516

commit v3 on v2

--- a/solution.py
+++ b/solution.py
@@ -83,13 +83,13 @@
 
     def transpose(k, _):
         o = pl.multiple_of(k * XB, XB)
-        xt[pl.ds(o, XB), :] = x_ref[:, pl.ds(o, XB)].T
+        xt[pl.ds(o, XB), :] = (x_ref[:, pl.ds(o, XB)] * inverse).astype(BF16).T
         return 0
 
     lax.fori_loop(0, D // XB, transpose, 0)
     pl.semaphore_wait(barrier, len(peers))
 
-    NB = pick(F, (512, 256, 128))
+    NB = pick(F, (256, 128))
 
     def r1_copy(cc):
         return remote(chg.at[cc, 1 - core], r1.at[cc], r1s.at[cc], r1r.at[cc], partner)
@@ -105,13 +105,13 @@
 
         def tile(n, _):
             o = pl.multiple_of(n * NB, NB)
-            g = jnp.dot(left, g_ref[:, pl.ds(o, NB)], preferred_element_type=F32) * inverse
+            g = jnp.dot(left, g_ref[:, pl.ds(o, NB)], preferred_element_type=F32)
             ch = g - stream[slot, pl.ds(0, R), pl.ds(o, NB)].astype(F32)
             acc[...] += (ch * ch).reshape(R // 8, 8, NB).sum(0)
             chg[cc, par, :, pl.ds(o, NB)] = ch.astype(BF16)
             return 0
 
-        lax.fori_loop(0, F // NB, tile, 0)
+        lax.fori_loop(0, F // NB, tile, 0, unroll=True)
         if send:
             r1_copy(cc).start()
 
@@ -213,13 +213,12 @@
         b1c[k, j] = remote(half_of(cc, 1), b1.at[n], b1s.at[n], b1r.at[n], peer(chip_at(x, y + k)))
         b1c[k, j].start()
 
-    order_a = [(k, j) for j in list(range(1, NY)) + [0] for k in range(1, NX)]
-    order_b = [(k, j) for j in list(range(1, NX)) + [0] for k in range(1, NY)]
-    for n in range(max(len(order_a), len(order_b))):
-        if n < len(order_a):
-            send_a1(*order_a[n])
-        if n < len(order_b):
-            send_b1(*order_b[n])
+    for j in range(1, NY):
+        for k in range(1, NX):
+            send_a1(k, j)
+    for j in range(1, NX):
+        for k in range(1, NY):
+            send_b1(k, j)
 
     def z_copy(owner, h):
         nxt = jnp.where(owner > t, t + 1, t - 1)
@@ -279,7 +278,12 @@
 
     lax.fori_loop(2 * (T - 1), 2 * T, pi_last, 0)
 
-    for u in range(1, T - 1):
+    for k in range(1, NX):
+        send_a1(k, 0)
+    for k in range(1, NY):
+        send_b1(k, 0)
+
+    def z_step(u):
         right = T - 1 - (u - t)
         left = u - (T - 1 - t)
 
@@ -290,6 +294,8 @@
         @pl.when((t < T - 1) & (left >= 0) & (left < t))
         def _():
             z_relay(left)
+
+    z_step(1)
 
     for j in range(1, NY):
         for k in range(1, NX):
@@ -306,6 +312,9 @@
         b2c[j] = remote(half_of(cc, 1), b2.at[j - 1], b2s.at[j - 1], b2r.at[j - 1], peer(cc))
         b2c[j].start()
 
+    for u in range(2, T - 1):
+        z_step(u)
+
     @pl.when(t > 0)
     def _():
         for h in range(2):
@@ -348,7 +357,7 @@
     R = D // (2 * NC)
     CH = D // T // 2
     FH = F // 2
-    NB = pick(F, (512, 256, 128))
+    NB = pick(F, (256, 128))
     nA, nB = (NX - 1) * NY, (NY - 1) * NX
     vmem = pl.BlockSpec(memory_space=pltpu.VMEM)
     hbm = pl.BlockSpec(memory_space=pl.ANY)

time: 137 us -> 132 us (0.964)
  Pallas kernels: 110 us -> 105 us
    pallas_call x1, Pallas kernels: 110 us -> 105 us  [body(): pl.pallas_call(functools.partial(kernel, cfg), out_shape=(jax.ShapeDtypeS...]
where the time goes in v3:
time: 132 us
  Pallas kernels  105 us (80%)
  matrix products  17.8 us (13%)
  other arithmetic  5.88 us (4%)
  local copies, waits for them, and re-layouts  2.12 us (2%)
    pallas_call x1, Pallas kernels, body(): pl.pallas_call(functools.partial(kernel, cfg), out_shape=(jax.ShapeDtypeS...  105 us
    dot_general x1, matrix products, body(): gate = jnp.dot(tokens, gate_weight, preferred_element_type=F32)  17.8 us
    add x1, other arithmetic, body(): return (aggregate + summed.astype(F32), input_grad, rms[0, 0:1])  5.88 us

profile of v3, /device:TPU:0, one launch (start us, length us, event | category | flops | bytes accessed | tf_op | source)
XLA Modules:
  0.0 131.6 jit_solution(12282769534129239853)
XLA Ops:
  1.3 17.8 %multiply_convert_fusion.g_ref = bf16[512,2560]{1,0:T(8,128)(2,1)} fusion(bf16[512,2560]{1,0:T(8,128)(2,1)} %param.9, bf16[512,2560]{1,0:T(8,128)(2,1)} %param.10, bf16[512,3584]{1,0:T(8,128)(2,1)} %x_ref.1, bf16[3584,2560]{1,0:T(8,128)(2,1)} %w_ref.1), kind=kOutput, calls=%fused_computation | convolution fusion | flops 9410969600 | bytes 29884416 | tf_op jit(solution)/shard_map/dot_general | solution.py:351
  19.1 104.6 %shard_map.94 = (bf16[448,2560]{1,0:T(8,128)(2,1)}, bf16[512,896]{1,0:T(8,128)(2,1)}, f32[8,128]{1,0:T(8,128)}) custom-call(bf16[512,3584]{1,0:T(8,128)(2,1)} %x_ref.1, bf16[512,2560]{1,0:T(8,128)(2,1)} %multiply_convert_fusion.g_ref, s32[1]{0:T(128)S(6)} %copy.11.mask_ref, bf16[1,3584,2560]{2,1,0:T(8,128)(2,1)} %lag_ref.1, bf16[3584,2560]{1,0:T(8,128)(2,1)} %w_ref.1), custom_call_target="tpu_custom_call" | custom-call | tf_op jit(solution)/shard_map/pallas_call | solution.py:365
  123.7 1.2 slice.3
  124.8 0.0 copy-start
  124.8 5.9 %convert_add_fusion = f32[448,2560]{1,0:T(8,128)} fusion(f32[448,2560]{1,0:T(8,128)} %param.13, bf16[448,2560]{1,0:T(8,128)(2,1)} %get-tuple-element.6), kind=kLoop, calls=%fused_computation.1 | loop fusion | flops 2293760 | bytes 11468800 | tf_op jit(solution)/shard_map/add | solution.py:401
  130.7 0.0 copy-done
  130.7 0.9 copy.12
Async XLA Ops:
  124.8 5.9 %copy-start = (bf16[512,896]{1,0:T(8,128)(2,1)S(1)}, bf16[512,896]{1,0:T(8,128)(2,1)}, u32[]{:S(2)}) copy-start(bf16[512,896]{1,0:T(8,128)(2,1)} %get-tuple-element.13) | copy-start | bytes 2752516
